TPU v7x, 32 devices: a whole 2x2x4 slice. The times are simulated.
32 devices in a mesh: band: 8 (over z, y), mode: 4 (over x, core).
Axes of the slice: x: 2, y: 2, z: 4, core: 2. Of those that a mesh axis runs over, the one named last changes fastest.
Arguments:
- velocity: bfloat16 [1, 8192, 1024], P(None, ('band', 'mode')), may hold values from -6 to 6
- radiation_modes: bfloat16 [8192, 1024], P('band', 'mode'), may hold values from -0.125 to 0.125
- resistance: float32 [8, 1024, 1024], P('band', None, 'mode'), as said below
- mode_ranks: int32 [8], P('band'), may hold values from 128 to 1024, as said below
- freq_table: int32 [512], replicated, may hold values from 0 to 511, each once
Outputs:
- adjoint_force: bfloat16 [1, 8192, 1024], P(None, ('band', 'mode'))
Inputs may be any that keep to these rules, and one draw needn't show every extreme that they name: `resistance`: each band's matrix is symmetric. `mode_ranks`: the ranks never fall with the band index; the first band keeps 1024 // 8 modes and the last 1024.
All inputs are finite; a program needn't handle non-finite values.
Results may differ from a plain program's by a relative error of at most 0.015.
Values may be sent and summed in bfloat16 or wider, within the bound.
A program may use at most 64 MiB of HBM per device.

v0:
```python
import functools
import math

import jax
import jax.numpy as jnp
from jax import lax
from jax.experimental import pallas as pl
from jax.experimental.pallas import tpu as pltpu
from jax.sharding import PartitionSpec as P

MESH = pl.DeviceIdType.MESH
HALF_ROWS = 32


def cosine_of(phase, period):
    wrapped = phase & (period - 1)
    folded = jnp.minimum(wrapped, period - wrapped)
    flip = folded > period // 4
    folded = jnp.where(flip, period // 2 - folded, folded)
    x = folded.astype(jnp.float32) * (2.0 * math.pi / period)
    y = x * x
    value = jnp.full_like(y, 1.0 / math.factorial(16))
    for n in range(14, -1, -2):
        sign = -1.0 if n % 4 else 1.0
        value = value * y + sign / math.factorial(n)
    return jnp.where(flip, -value, value)


def fused_kernel(
    nb, nm, vel_ref, modes_ref, res_ref, rank_ref, freq_ref, out_ref,
    table, trig, modes_t, res_hi, res_lo, spec, part, rs, coef, force, basis, acc,
    sx_s, sx_r, sm_s, sm_r, sf_s, sf_r, rs_s, rs_r, k_s, k_r, ob_s, ob_r,
    fz_s, fz_r, fy_s, fy_r, fx_s, fx_r, gy_s, gy_r, gx_s, gx_r, fm_s, fm_r, ff_s, ff_r,
):
    b = lax.axis_index("band")
    m = lax.axis_index("mode")
    mate = m + 1 - 2 * (m % 2)
    cross = (m + 2) % nm
    diag = (mate + 2) % nm
    patches, steps = vel_ref.shape
    cols = table.shape[2]
    mode_cols = modes_ref.shape[1]

    def band_at(e):
        bits = [1 << i for i in range(nb.bit_length() - 1)]
        return sum(bit * ((b // bit + e // bit) % 2) for bit in bits)

    def to_mode(src, dst, send, recv, target):
        return pltpu.make_async_remote_copy(
            src_ref=src, dst_ref=dst, send_sem=send, recv_sem=recv,
            device_id={"mode": target}, device_id_type=MESH)

    def to_band(src, dst, send, recv, target):
        return pltpu.make_async_remote_copy(
            src_ref=src, dst_ref=dst, send_sem=send, recv_sem=recv,
            device_id={"band": target}, device_id_type=MESH)

    barrier = pltpu.get_barrier_semaphore()
    for off in range(1, nm):
        pl.semaphore_signal(barrier, inc=1, device_id={"mode": (m + off) % nm}, device_id_type=MESH)
    for off in range(1, nb):
        pl.semaphore_signal(barrier, inc=1, device_id={"band": band_at(off)}, device_id_type=MESH)

    blocks = steps // HALF_ROWS
    norming = 1.0 / math.sqrt(steps)

    def build(k):
        half = cols // 2
        lane = lax.broadcasted_iota(jnp.int32, (HALF_ROWS, cols), 1)
        row = jnp.broadcast_to(freq_ref[pl.ds(k // 2, 1), :], (HALF_ROWS, cols))
        freq = jnp.where(lane // half == k % 2, row, pltpu.roll(row, half, 1))
        shift = jnp.where(lane < half, 0, steps // 4)
        rows = lax.broadcasted_iota(jnp.int32, (HALF_ROWS, cols), 0)
        big = lax.broadcasted_iota(jnp.int32, (blocks, cols), 0) * HALF_ROWS
        low = rows * freq + shift
        high = big * freq
        quarter = steps // 4
        cos_low = cosine_of(low, steps) * norming
        sin_low = cosine_of(low - quarter, steps) * norming
        trig[0] = cosine_of(high, steps)
        trig[1] = cosine_of(high - quarter, steps)
        for a in range(blocks):
            row = trig[0, pl.ds(a, 1), :] * cos_low - trig[1, pl.ds(a, 1), :] * sin_low
            table[k, pl.ds(a * HALF_ROWS, HALF_ROWS), :] = row.astype(jnp.bfloat16)

    def spectra(k):
        build(k)
        spec[k, m] = jnp.dot(
            vel_ref[...], table[k], preferred_element_type=jnp.float32
        ).astype(jnp.bfloat16)

    spectra(band_at(nb - 1))
    modes_t[...] = modes_ref[...].T
    wide = res_ref[...].T
    narrow = wide.astype(jnp.bfloat16)
    res_hi[...] = narrow
    res_lo[...] = (wide - narrow.astype(jnp.float32)).astype(jnp.bfloat16)
    pl.semaphore_wait(barrier, nm - 1 + nb - 1)

    def s_cross(k):
        return to_mode(spec.at[k, m], spec.at[k, m], sx_s.at[k], sx_r.at[k], cross)

    def s_mate(k):
        return to_mode(spec.at[k, m], spec.at[k, m], sm_s.at[k], sm_r.at[k], mate)

    def s_fwd(k):
        return to_mode(spec.at[k, cross], spec.at[k, cross], sf_s.at[k], sf_r.at[k], mate)

    def spec_step(i, _):
        k = band_at(nb - 1 - i)
        s_cross(k).start()
        s_mate(k).start()
        spectra(band_at(nb - 2 - i))
        return 0

    lax.fori_loop(0, nb - 1, spec_step, 0)
    s_cross(b).start()
    s_mate(b).start()

    def basis_copy(off):
        target = (m + off) % nm
        rows = pl.ds(pl.multiple_of(target * patches, patches), patches)
        return to_mode(modes_ref.at[rows], basis.at[m], ob_s.at[off], ob_r.at[off], target)

    for off in range(1, nm):
        basis_copy(off).start()
    def partial(k):
        return jnp.dot(
            modes_t[...], spec[k].reshape(nm * patches, cols), preferred_element_type=jnp.float32)

    def rs_copy(k):
        return to_band(part.at[k], rs.at[b], rs_s.at[k], rs_r.at[b], k)

    def rs_arrival(k):
        return to_band(part.at[k], rs.at[k], rs_s.at[k], rs_r.at[k], k)

    def arrive(k):
        s_cross(k).wait_recv()
        s_fwd(k).start()

    def finish(k):
        s_mate(k).wait_recv()
        s_fwd(k).wait_recv()

    def part_step(i, _):
        k = band_at(nb - 1 - i)
        arrive(band_at(nb - 2 - i))
        finish(k)
        part[k] = partial(k).astype(jnp.bfloat16)
        rs_copy(k).start()
        return 0

    arrive(band_at(nb - 1))
    lax.fori_loop(0, nb - 1, part_step, 0)
    finish(b)
    total = partial(b)
    for off in range(1, nb):
        k = band_at(nb - off)
        rs_arrival(k).wait_recv()
        total = total + rs[k].astype(jnp.float32)
    kept = lax.broadcasted_iota(jnp.int32, (mode_cols, cols), 0) + m * mode_cols < rank_ref[...]
    total = jnp.where(kept, total, 0.0)
    coef[m] = total.astype(jnp.bfloat16)

    def k_copy(off):
        return to_mode(coef.at[m], coef.at[m], k_s.at[off], k_r.at[off], (m + off) % nm)

    def k_arrival(off):
        source = (m + nm - off) % nm
        return to_mode(coef.at[source], coef.at[source], k_s.at[off], k_r.at[off], source)

    for off in range(1, nm):
        k_copy(off).start()
    for off in range(1, nm):
        k_arrival(off).wait_recv()
    coefs = coef[...].reshape(nm * mode_cols, cols)
    forcing = jnp.dot(res_hi[...], coefs, preferred_element_type=jnp.float32) + jnp.dot(
        res_lo[...], coefs, preferred_element_type=jnp.float32)
    forcing = jnp.where(kept, 2.0 * forcing, 0.0)
    force[b, m] = forcing.astype(jnp.bfloat16)

    half = mode_cols // 2
    upper, lower = pl.ds(0, half), pl.ds(half, half)
    near = band_at(1)

    def f_far(k):
        return to_band(force.at[b, m], force.at[b, m], fz_s.at[k], fz_r.at[b], k)

    def f_far_arrival(k):
        return to_band(force.at[k, m], force.at[k, m], fz_s.at[k], fz_r.at[k], k)

    def f_near(k):
        return to_band(force.at[k, m], force.at[k, m], fy_s.at[k], fy_r.at[k], near)

    def f_cross(k):
        return to_mode(force.at[k, m], force.at[k, m], fx_s.at[k], fx_r.at[k], cross)

    def g_near(k):
        piece = force.at[k, cross, lower]
        return to_band(piece, piece, gy_s.at[k], gy_r.at[k], near)

    def g_cross(k):
        piece = force.at[k, m, upper]
        return to_mode(piece, piece, gx_s.at[k], gx_r.at[k], cross)

    def f_mate(k):
        return to_mode(force.at[k, m], force.at[k, m], fm_s.at[k], fm_r.at[k], mate)

    def f_fwd(k):
        return to_mode(force.at[k, cross], force.at[k, cross], ff_s.at[k], ff_r.at[k], mate)

    far = list(range(0, nb, 2))

    def first(j):
        k = band_at(far[j])
        if j > 0:
            f_far_arrival(k).wait_recv()
        f_near(k).start()
        f_cross(k).start()
        f_mate(k).start()

    def second(j):
        k, k1 = band_at(far[j]), band_at(far[j] + 1)
        f_near(k1).wait_recv()
        g_cross(k1).start()
        f_mate(k1).start()
        f_cross(k).wait_recv()
        g_near(k).start()
        f_fwd(k).start()

    def third(j):
        k1 = band_at(far[j] + 1)
        g_cross(k1).wait_recv()
        g_near(k1).wait_recv()
        f_fwd(k1).start()

    for e in far[1:]:
        f_far(band_at(e)).start()
    first(0)

    for off in range(1, nm):
        source = (m + nm - off) % nm
        to_mode(basis.at[source], basis.at[source], ob_s.at[off], ob_r.at[off], source).wait_recv()
    basis[m] = modes_ref[pl.ds(pl.multiple_of(m * patches, patches), patches), :]

    def surface(k):
        value = jnp.dot(basis[0], force[k, 0], preferred_element_type=jnp.float32)
        for j in range(1, nm):
            value = value + jnp.dot(basis[j], force[k, j], preferred_element_type=jnp.float32)
        return value.astype(jnp.bfloat16)

    def history(k):
        f_mate(k).wait_recv()
        f_fwd(k).wait_recv()
        return lax.dot_general(
            surface(k), table[k], (((1,), (1,)), ((), ())), preferred_element_type=jnp.float32)

    def last(e):
        term = history(band_at(e))
        if e == 0:
            acc[...] = term
        elif e < nb - 1:
            acc[...] += term
        else:
            out_ref[...] = (acc[...] + term).astype(out_ref.dtype)

    n = len(far)
    for j in range(1, n):
        first(j)
    for j in range(n):
        second(j)
    for j in range(n - 1):
        last(far[j])
        third(j)
    third(n - 1)
    last(far[n - 1])
    for j in range(n):
        last(far[j] + 1)

    def drain(k, _):
        for copy in (s_cross, s_mate, s_fwd, f_mate, f_fwd):
            copy(k).wait_send()
        return 0

    lax.fori_loop(0, nb, drain, 0)
    for off in range(1, nb):
        k = band_at(off)
        rs_copy(k).wait_send()
    for e in far:
        k, k1 = band_at(e), band_at(e + 1)
        if e > 0:
            f_far(k).wait_send()
        f_near(k).wait_send()
        f_cross(k).wait_send()
        g_near(k).wait_send()
        g_cross(k1).wait_send()
    for off in range(1, nm):
        basis_copy(off).wait_send()
        k_copy(off).wait_send()


def fused(mesh, velocity, radiation_modes, resistance, mode_ranks, freq_table):
    nb, nm = mesh.shape["band"], mesh.shape["mode"]
    patches, steps = velocity.shape[1:]
    mode_cols = radiation_modes.shape[1]
    modes = nm * mode_cols
    cols = 2 * (freq_table.shape[0] // nb)
    bf16, f32 = jnp.bfloat16, jnp.float32
    dma = lambda n: pltpu.SemaphoreType.DMA((n,))
    vmem = pl.BlockSpec(memory_space=pltpu.VMEM)
    out = pl.pallas_call(
        functools.partial(fused_kernel, nb, nm),
        out_shape=jax.ShapeDtypeStruct((patches, steps), bf16),
        in_specs=[vmem] * 5,
        out_specs=vmem,
        scratch_shapes=[
            pltpu.VMEM((nb, steps, cols), bf16),
            pltpu.VMEM((2, steps // HALF_ROWS, cols), f32),
            pltpu.VMEM((mode_cols, nm * patches), bf16),
            pltpu.VMEM((mode_cols, modes), bf16),
            pltpu.VMEM((mode_cols, modes), bf16),
            pltpu.VMEM((nb, nm, patches, cols), bf16),
            pltpu.VMEM((nb, mode_cols, cols), bf16),
            pltpu.VMEM((nb, mode_cols, cols), bf16),
            pltpu.VMEM((nm, mode_cols, cols), bf16),
            pltpu.VMEM((nb, nm, mode_cols, cols), bf16),
            pltpu.VMEM((nm, patches, mode_cols), bf16),
            pltpu.VMEM((patches, steps), f32),
            ]
        + [dma(nb) for _ in range(8)]
        + [dma(nm) for _ in range(4)]
        + [dma(nb) for _ in range(14)],
        compiler_params=pltpu.CompilerParams(collective_id=0, has_side_effects=True),
    )(velocity[0], radiation_modes, resistance[0], mode_ranks.reshape(1, 1), freq_table.reshape(nb // 2, cols))
    return out[None]


def make_table(freq_table, step_count):
    times = jnp.arange(step_count, dtype=jnp.int32)
    phases = times[:, None] * freq_table[None, :] % step_count
    angles = phases.astype(jnp.float32) * (2.0 * math.pi / step_count)
    norming = 1.0 / math.sqrt(step_count)
    table = jnp.stack([jnp.cos(angles), -jnp.sin(angles)], axis=1) * norming
    return table.astype(jnp.bfloat16)


def add_sources(received):
    return jnp.sum(received, axis=0)


def per_device(velocity, radiation_modes, resistance, mode_ranks, freq_table):
    step_count = velocity.shape[2]
    mode_cols = radiation_modes.shape[1]
    dft_table = make_table(freq_table, step_count)
    spectra = jnp.einsum(
        "wpt,tcf->wpcf", velocity, dft_table, preferred_element_type=jnp.float32
    ).astype(jnp.bfloat16)
    partial_value = jnp.einsum(
        "wpcf,pr->wrcf",
        lax.all_gather(spectra, "mode", axis=1, tiled=True),
        radiation_modes,
        preferred_element_type=jnp.float32,
    )
    coefficients = add_sources(
        lax.all_to_all(
            partial_value[None].astype(jnp.bfloat16),
            "band",
            split_axis=4,
            concat_axis=0,
            tiled=True,
        ).astype(jnp.float32)
    )
    offset = lax.axis_index("mode") * mode_cols
    rank_here = mode_ranks[0]
    kept_mask = (offset + jnp.arange(mode_cols, dtype=jnp.int32) < rank_here).astype(jnp.float32)
    kept_mask = kept_mask[None, :, None, None]
    coefficients = coefficients * kept_mask
    matrix = resistance[0]
    partial_terms = jnp.einsum(
        "ij,wjcf->wicf", matrix, coefficients, precision=lax.Precision.HIGHEST
    )
    forcing = lax.psum_scatter(
        partial_terms.astype(jnp.bfloat16), "mode", scatter_dimension=1, tiled=True
    ).astype(jnp.float32)
    forcing = (2.0 * forcing * kept_mask).astype(jnp.bfloat16)
    collected = lax.all_gather(forcing, "mode", axis=1, tiled=True)
    collected = lax.all_gather(collected, "band", axis=3, tiled=True)
    own_basis = lax.all_to_all(radiation_modes, "mode", split_axis=0, concat_axis=1, tiled=True)
    surface_force = jnp.einsum(
        "pr,wrcf->wpcf", own_basis, collected, preferred_element_type=jnp.float32
    ).astype(jnp.bfloat16)
    history = jnp.einsum(
        "wpcf,tcf->wpt", surface_force, dft_table, preferred_element_type=jnp.float32
    )
    return history.astype(jnp.bfloat16)


def solution(mesh):
    placed = (
        P(None, ("band", "mode"), None),
        P("band", "mode"),
        P("band", None, "mode"),
        P("band"),
        P(),
    )
    nb, nm = mesh.shape["band"], mesh.shape["mode"]

    def body(velocity, radiation_modes, resistance, mode_ranks, freq_table):
        windows, patches, steps = velocity.shape
        mode_cols = radiation_modes.shape[1]
        cols = 2 * (freq_table.shape[0] // nb)
        tiled = (
            windows == 1 and nm == 4 and nb == 8 and cols == 128 and mode_cols % 128 == 0
            and patches % 128 == 0 and steps % 128 == 0 and steps & (steps - 1) == 0
        )
        args = (velocity, radiation_modes, resistance, mode_ranks, freq_table)
        return fused(mesh, *args) if tiled else per_device(*args)

    return jax.shard_map(
        body,
        mesh=mesh,
        in_specs=placed,
        out_specs=P(None, ("band", "mode"), None),
        check_vma=False,
    )
```

profile of v0, /device:TPU:0, one launch (start us, length us, event | category | flops | bytes accessed | tf_op | source)
XLA Modules:
  0.0 52.8 jit_solution(4209343914937591640)
XLA Ops:
  0.7 50.3 %shard_map.55 = bf16[256,1024]{1,0:T(8,128)(2,1)} custom-call(bf16[256,1024]{1,0:T(8,128)(2,1)} %bitcast.8, bf16[1024,256]{1,0:T(8,128)(2,1)} %modes_ref.1, f32[1024,256]{1,0:T(8,128)} %bitcast.7, s32[1,1]{1,0:T(1,128)} %bitcast.5.rank_ref, s32[4,128]{1,0:T(4,128)} %bitcast.9), custom_call_target="tpu_custom_call" | custom-call | tf_op jit(solution)/shard_map/pallas_call | solution.py:311
  51.0 1.9 %copy.8 = bf16[1,256,1024]{2,1,0:T(8,128)(2,1)} copy(bf16[1,256,1024]{2,1,0:T(8,128)(2,1)} %bitcast.6) | data formatting | bytes 1048576
where the time goes:
time: 53 us; the launch traced here: 52.8 us
  Pallas kernels  50.3 us (95%)
  local copies, waits for them, and re-layouts  1.87 us (4%)
  between operations  0.66 us (1%)
    pallas_call x1, Pallas kernels, fused(): pl.pallas_call(functools.partial(fused_kernel, nb, nm), out_shape=jax.Sha...  50.3 us
    unnamed x1, local copies, waits for them, and re-layouts  1.87 us

commit v1 on v0

--- a/solution.py
+++ b/solution.py
@@ -27,9 +27,10 @@
 
 
 def fused_kernel(
-    nb, nm, vel_ref, modes_ref, res_ref, rank_ref, freq_ref, out_ref,
-    table, trig, modes_t, res_hi, res_lo, spec, part, rs, coef, force, basis, acc,
-    sx_s, sx_r, sm_s, sm_r, sf_s, sf_r, rs_s, rs_r, k_s, k_r, ob_s, ob_r,
+    nb, nm, vel_hbm, modes_hbm, res_hbm, rank_hbm, freq_hbm, out_ref,
+    vel_ref, modes_ref, res_ref, rank_ref, freq_ref,
+    table, trig, modes_t, res_hi, res_lo, spec, part, pend, rs, coef, force, basis, acc,
+    in_s, sx_s, sx_r, sm_s, sm_r, sf_s, sf_r, ry_s, ry_r, rs_s, rs_r, k_s, k_r, ob_s, ob_r,
     fz_s, fz_r, fy_s, fy_r, fx_s, fx_r, gy_s, gy_r, gx_s, gx_r, fm_s, fm_r, ff_s, ff_r,
 ):
     b = lax.axis_index("band")
@@ -55,6 +56,14 @@
             src_ref=src, dst_ref=dst, send_sem=send, recv_sem=recv,
             device_id={"band": target}, device_id_type=MESH)
 
+    loads = [
+        pltpu.make_async_copy(src, dst, in_s.at[i])
+        for i, (src, dst) in enumerate((
+            (freq_hbm, freq_ref), (vel_hbm, vel_ref), (modes_hbm, modes_ref),
+            (res_hbm, res_ref), (rank_hbm, rank_ref)))
+    ]
+    for load in loads:
+        load.start()
     barrier = pltpu.get_barrier_semaphore()
     for off in range(1, nm):
         pl.semaphore_signal(barrier, inc=1, device_id={"mode": (m + off) % nm}, device_id_type=MESH)
@@ -83,81 +92,103 @@
             row = trig[0, pl.ds(a, 1), :] * cos_low - trig[1, pl.ds(a, 1), :] * sin_low
             table[k, pl.ds(a * HALF_ROWS, HALF_ROWS), :] = row.astype(jnp.bfloat16)
 
-    def spectra(k):
-        build(k)
+    def project(k):
         spec[k, m] = jnp.dot(
             vel_ref[...], table[k], preferred_element_type=jnp.float32
         ).astype(jnp.bfloat16)
 
-    spectra(band_at(nb - 1))
+    loads[0].wait()
+    build(band_at(nb - 1))
+    loads[1].wait()
+    project(band_at(nb - 1))
+    pl.semaphore_wait(barrier, nm - 1 + nb - 1)
+
+    def s_cross(k):
+        return to_mode(spec.at[k, m], spec.at[k, m], sx_s.at[k], sx_r.at[k], cross)
+
+    def s_mate(k):
+        return to_mode(spec.at[k, m], spec.at[k, m], sm_s.at[k], sm_r.at[k], mate)
+
+    def s_fwd(k):
+        return to_mode(spec.at[k, cross], spec.at[k, cross], sf_s.at[k], sf_r.at[k], mate)
+
+    def spec_step(i, _):
+        k = band_at(nb - 1 - i)
+        s_cross(k).start()
+        s_mate(k).start()
+        build(band_at(nb - 2 - i))
+        project(band_at(nb - 2 - i))
+        return 0
+
+    lax.fori_loop(0, nb - 1, spec_step, 0)
+    s_cross(b).start()
+    s_mate(b).start()
+
+    def basis_copy(off):
+        target = (m + off) % nm
+        rows = pl.ds(pl.multiple_of(target * patches, patches), patches)
+        return to_mode(modes_ref.at[rows], basis.at[m], ob_s.at[off], ob_r.at[off], target)
+
+    loads[2].wait()
+    for off in range(1, nm):
+        basis_copy(off).start()
     modes_t[...] = modes_ref[...].T
+    loads[3].wait()
     wide = res_ref[...].T
     narrow = wide.astype(jnp.bfloat16)
     res_hi[...] = narrow
     res_lo[...] = (wide - narrow.astype(jnp.float32)).astype(jnp.bfloat16)
-    pl.semaphore_wait(barrier, nm - 1 + nb - 1)
-
-    def s_cross(k):
-        return to_mode(spec.at[k, m], spec.at[k, m], sx_s.at[k], sx_r.at[k], cross)
-
-    def s_mate(k):
-        return to_mode(spec.at[k, m], spec.at[k, m], sm_s.at[k], sm_r.at[k], mate)
-
-    def s_fwd(k):
-        return to_mode(spec.at[k, cross], spec.at[k, cross], sf_s.at[k], sf_r.at[k], mate)
-
-    def spec_step(i, _):
-        k = band_at(nb - 1 - i)
-        s_cross(k).start()
-        s_mate(k).start()
-        spectra(band_at(nb - 2 - i))
-        return 0
-
-    lax.fori_loop(0, nb - 1, spec_step, 0)
-    s_cross(b).start()
-    s_mate(b).start()
-
-    def basis_copy(off):
-        target = (m + off) % nm
-        rows = pl.ds(pl.multiple_of(target * patches, patches), patches)
-        return to_mode(modes_ref.at[rows], basis.at[m], ob_s.at[off], ob_r.at[off], target)
-
-    for off in range(1, nm):
-        basis_copy(off).start()
+    loads[4].wait()
+
     def partial(k):
         return jnp.dot(
             modes_t[...], spec[k].reshape(nm * patches, cols), preferred_element_type=jnp.float32)
 
-    def rs_copy(k):
-        return to_band(part.at[k], rs.at[b], rs_s.at[k], rs_r.at[b], k)
-
-    def rs_arrival(k):
-        return to_band(part.at[k], rs.at[k], rs_s.at[k], rs_r.at[k], k)
-
-    def arrive(k):
+    near = band_at(1)
+    pairs = nb // 2
+
+    def y_copy(j):
+        k = band_at(2 * j + 1)
+        return to_band(part.at[k], rs.at[j], ry_s.at[j], ry_r.at[j], near)
+
+    def z_copy(j):
+        k = band_at(2 * j)
+        return to_band(part.at[k], rs.at[pairs + j], rs_s.at[j], rs_r.at[j], k)
+
+    def gather(k):
         s_cross(k).wait_recv()
         s_fwd(k).start()
-
-    def finish(k):
         s_mate(k).wait_recv()
         s_fwd(k).wait_recv()
+        return partial(k)
+
+    def away(j):
+        k = band_at(2 * j + 1)
+        part[k] = gather(k).astype(jnp.bfloat16)
+        y_copy(j).start()
+
+    def pass_on(j):
+        y_copy(j).wait_recv()
+        part[band_at(2 * j)] = (pend[...] + rs[j].astype(jnp.float32)).astype(jnp.bfloat16)
+        z_copy(j).start()
+
+    away(pairs - 1)
+    pend[...] = gather(band_at(nb - 2))
 
     def part_step(i, _):
-        k = band_at(nb - 1 - i)
-        arrive(band_at(nb - 2 - i))
-        finish(k)
-        part[k] = partial(k).astype(jnp.bfloat16)
-        rs_copy(k).start()
+        j = pairs - 2 - i
+        away(j)
+        pass_on(j + 1)
+        pend[...] = gather(band_at(2 * j))
         return 0
 
-    arrive(band_at(nb - 1))
-    lax.fori_loop(0, nb - 1, part_step, 0)
-    finish(b)
-    total = partial(b)
-    for off in range(1, nb):
-        k = band_at(nb - off)
-        rs_arrival(k).wait_recv()
-        total = total + rs[k].astype(jnp.float32)
+    lax.fori_loop(0, pairs - 1, part_step, 0)
+    total = pend[...]
+    for j in range(pairs - 1, 0, -1):
+        z_copy(j).wait_recv()
+        total = total + rs[pairs + j].astype(jnp.float32)
+    y_copy(0).wait_recv()
+    total = total + rs[0].astype(jnp.float32)
     kept = lax.broadcasted_iota(jnp.int32, (mode_cols, cols), 0) + m * mode_cols < rank_ref[...]
     total = jnp.where(kept, total, 0.0)
     coef[m] = total.astype(jnp.bfloat16)
@@ -181,7 +212,6 @@
 
     half = mode_cols // 2
     upper, lower = pl.ds(0, half), pl.ds(half, half)
-    near = band_at(1)
 
     def f_far(k):
         return to_band(force.at[b, m], force.at[b, m], fz_s.at[k], fz_r.at[b], k)
@@ -269,13 +299,15 @@
         first(j)
     for j in range(n):
         second(j)
-    for j in range(n - 1):
+    last(0)
+    third(0)
+    for j in range(1, n):
         last(far[j])
+        if j > 1:
+            last(far[j] - 3)
         third(j)
-    third(n - 1)
-    last(far[n - 1])
-    for j in range(n):
-        last(far[j] + 1)
+    last(far[n - 1] - 1)
+    last(far[n - 1] + 1)
 
     def drain(k, _):
         for copy in (s_cross, s_mate, s_fwd, f_mate, f_fwd):
@@ -283,9 +315,10 @@
         return 0
 
     lax.fori_loop(0, nb, drain, 0)
-    for off in range(1, nb):
-        k = band_at(off)
-        rs_copy(k).wait_send()
+    for j in range(pairs):
+        y_copy(j).wait_send()
+        if j > 0:
+            z_copy(j).wait_send()
     for e in far:
         k, k1 = band_at(e), band_at(e + 1)
         if e > 0:
@@ -308,12 +341,18 @@
     bf16, f32 = jnp.bfloat16, jnp.float32
     dma = lambda n: pltpu.SemaphoreType.DMA((n,))
     vmem = pl.BlockSpec(memory_space=pltpu.VMEM)
+    hbm = pl.BlockSpec(memory_space=pltpu.HBM)
     out = pl.pallas_call(
         functools.partial(fused_kernel, nb, nm),
-        out_shape=jax.ShapeDtypeStruct((patches, steps), bf16),
-        in_specs=[vmem] * 5,
+        out_shape=pltpu.VMEM((patches, steps), bf16),
+        in_specs=[hbm] * 5,
         out_specs=vmem,
         scratch_shapes=[
+            pltpu.VMEM((patches, steps), bf16),
+            pltpu.VMEM(radiation_modes.shape, bf16),
+            pltpu.VMEM(resistance.shape[1:], f32),
+            pltpu.VMEM((1, 1), jnp.int32),
+            pltpu.VMEM((nb // 2, cols), jnp.int32),
             pltpu.VMEM((nb, steps, cols), bf16),
             pltpu.VMEM((2, steps // HALF_ROWS, cols), f32),
             pltpu.VMEM((mode_cols, nm * patches), bf16),
@@ -321,13 +360,15 @@
             pltpu.VMEM((mode_cols, modes), bf16),
             pltpu.VMEM((nb, nm, patches, cols), bf16),
             pltpu.VMEM((nb, mode_cols, cols), bf16),
+            pltpu.VMEM((mode_cols, cols), f32),
             pltpu.VMEM((nb, mode_cols, cols), bf16),
             pltpu.VMEM((nm, mode_cols, cols), bf16),
             pltpu.VMEM((nb, nm, mode_cols, cols), bf16),
             pltpu.VMEM((nm, patches, mode_cols), bf16),
             pltpu.VMEM((patches, steps), f32),
             ]
-        + [dma(nb) for _ in range(8)]
+        + [dma(5)]
+        + [dma(nb) for _ in range(10)]
         + [dma(nm) for _ in range(4)]
         + [dma(nb) for _ in range(14)],
         compiler_params=pltpu.CompilerParams(collective_id=0, has_side_effects=True),

time: 53 us -> 48.2 us (0.909)
  Pallas kernels: 50.3 us -> 46.6 us
  local copies, waits for them, and re-layouts: 1.87 us -> 0.8 us
    pallas_call x1, Pallas kernels: 50.3 us -> 46.6 us  [fused(): pl.pallas_call(functools.partial(fused_kernel, nb, nm), out_shape=pltpu.V...]
    unnamed x1, local copies, waits for them, and re-layouts: 1.87 us -> 0.8 us
where the time goes in v1:
time: 48.2 us; the launch traced here: 48 us
  Pallas kernels  46.6 us (97%)
  local copies, waits for them, and re-layouts  0.8 us (2%)
  between operations  0.66 us (1%)
    pallas_call x1, Pallas kernels, fused(): pl.pallas_call(functools.partial(fused_kernel, nb, nm), out_shape=pltpu.V...  46.6 us

profile of v1, /device:TPU:0, one launch (start us, length us, event | category | flops | bytes accessed | tf_op | source)
XLA Modules:
  0.0 48.0 jit_solution(12301084293678078924)
XLA Ops:
  0.7 46.6 %shard_map.55 = bf16[256,1024]{1,0:T(8,128)(2,1)S(1)} custom-call(bf16[256,1024]{1,0:T(8,128)(2,1)} %bitcast.8, bf16[1024,256]{1,0:T(8,128)(2,1)} %modes_hbm.1, f32[1024,256]{1,0:T(8,128)} %bitcast.7, s32[1,1]{1,0:T(1,128)} %bitcast.5.rank_hbm, s32[4,128]{1,0:T(4,128)} %bitcast.9), custom_call_target="tpu_custom_call" | custom-call | tf_op jit(solution)/shard_map/pallas_call | solution.py:345
  47.2 0.8 %copy.7 = bf16[1,256,1024]{2,1,0:T(8,128)(2,1)} copy(bf16[1,256,1024]{2,1,0:T(8,128)(2,1)S(1)} %bitcast.6) | data formatting | bytes 1048576

commit v2 on v1

v2 whole, which is shorter than its diff:
```python
import functools
import math

import jax
import jax.numpy as jnp
from jax import lax
from jax.experimental import pallas as pl
from jax.experimental.pallas import tpu as pltpu
from jax.sharding import PartitionSpec as P

MESH = pl.DeviceIdType.MESH
HALF_ROWS = 32


def cosine_of(phase, period):
    wrapped = phase & (period - 1)
    folded = jnp.minimum(wrapped, period - wrapped)
    flip = folded > period // 4
    folded = jnp.where(flip, period // 2 - folded, folded)
    x = folded.astype(jnp.float32) * (2.0 * math.pi / period)
    y = x * x
    value = jnp.full_like(y, 1.0 / math.factorial(16))
    for n in range(14, -1, -2):
        sign = -1.0 if n % 4 else 1.0
        value = value * y + sign / math.factorial(n)
    return jnp.where(flip, -value, value)


def fused_kernel(
    nb, nm, vel_hbm, modes_hbm, res_hbm, rank_hbm, freq_hbm, out_ref,
    vel_ref, modes_ref, res_ref, rank_ref, freq_ref,
    table, trig, modes_t, res_t, spec, part, pend, summed, coef, force, basis, acc,
    in_s, tx, sx_r, sm_r, sf_r, ry_r, rz_r, k_r, ob_r,
    far_r, nu_r, nl_r, cu_r, cl_r, g_r, mf_r,
):
    b = lax.axis_index("band")
    m = lax.axis_index("mode")
    mate = m + 1 - 2 * (m % 2)
    cross = (m + 2) % nm
    here = m // 2
    patches, steps = vel_ref.shape
    cols = table.shape[2]
    mode_cols = modes_ref.shape[1]
    pairs = nb // 2

    def band_at(e):
        bits = [1 << i for i in range(nb.bit_length() - 1)]
        return sum(bit * ((b // bit + e // bit) % 2) for bit in bits)

    near = band_at(1)

    def to_mode(src, dst, send, recv, target):
        return pltpu.make_async_remote_copy(
            src_ref=src, dst_ref=dst, send_sem=tx.at[send], recv_sem=recv,
            device_id={"mode": target}, device_id_type=MESH)

    def to_band(src, dst, send, recv, target):
        return pltpu.make_async_remote_copy(
            src_ref=src, dst_ref=dst, send_sem=tx.at[send], recv_sem=recv,
            device_id={"band": target}, device_id_type=MESH)

    def wait_bytes(ref, sem):
        pltpu.make_async_copy(ref, ref, sem).wait()

    loads = [
        pltpu.make_async_copy(src, dst, in_s.at[i])
        for i, (src, dst) in enumerate((
            (freq_hbm, freq_ref), (vel_hbm, vel_ref), (modes_hbm, modes_ref),
            (res_hbm, res_ref), (rank_hbm, rank_ref)))
    ]
    for load in loads:
        load.start()
    barrier = pltpu.get_barrier_semaphore()
    for off in range(1, nm):
        pl.semaphore_signal(barrier, inc=1, device_id={"mode": (m + off) % nm}, device_id_type=MESH)
    for off in range(1, nb):
        pl.semaphore_signal(barrier, inc=1, device_id={"band": band_at(off)}, device_id_type=MESH)

    blocks = steps // HALF_ROWS
    norming = 1.0 / math.sqrt(steps)

    def build(k):
        half = cols // 2
        lane = lax.broadcasted_iota(jnp.int32, (HALF_ROWS, cols), 1)
        row = jnp.broadcast_to(freq_ref[pl.ds(k // 2, 1), :], (HALF_ROWS, cols))
        freq = jnp.where(lane // half == k % 2, row, pltpu.roll(row, half, 1))
        shift = jnp.where(lane < half, 0, steps // 4)
        rows = lax.broadcasted_iota(jnp.int32, (HALF_ROWS, cols), 0)
        big = lax.broadcasted_iota(jnp.int32, (blocks, cols), 0) * HALF_ROWS
        low = rows * freq + shift
        high = big * freq
        quarter = steps // 4
        cos_low = cosine_of(low, steps) * norming
        sin_low = cosine_of(low - quarter, steps) * norming
        trig[0] = cosine_of(high, steps)
        trig[1] = cosine_of(high - quarter, steps)
        for a in range(blocks):
            row = trig[0, pl.ds(a, 1), :] * cos_low - trig[1, pl.ds(a, 1), :] * sin_low
            table[k, pl.ds(a * HALF_ROWS, HALF_ROWS), :] = row.astype(jnp.bfloat16)

    def project(k):
        spec[k, m] = jnp.dot(
            vel_ref[...], table[k], preferred_element_type=jnp.float32
        ).astype(jnp.bfloat16)

    order = (7, 5, 6, 3, 4, 1, 2, 0)

    def slot(i):
        return band_at(order[i])

    def s_cross(k):
        return to_mode(spec.at[k, m], spec.at[k, m], 0, sx_r.at[k], cross)

    def s_mate(k):
        return to_mode(spec.at[k, m], spec.at[k, m], 0, sm_r.at[0], mate)

    def s_fwd(k):
        return to_mode(spec.at[k, cross], spec.at[k, cross], 0, sf_r.at[k], mate)

    loads[0].wait()
    build(slot(0))
    loads[1].wait()
    project(slot(0))
    pl.semaphore_wait(barrier, nm - 1 + nb - 1)

    for i in range(nb):
        s_cross(slot(i)).start()
        s_mate(slot(i)).start()
        if i < nb - 1:
            build(slot(i + 1))
            project(slot(i + 1))

    def basis_copy(off):
        target = (m + off) % nm
        rows = pl.ds(pl.multiple_of(target * patches, patches), patches)
        return to_mode(modes_ref.at[rows], basis.at[m], 3, ob_r.at[0], target)

    loads[2].wait()
    for off in range(1, nm):
        basis_copy(off).start()
    for half in range(2):
        rows = pl.ds(pl.multiple_of(((here + half) % 2) * 2 * patches, 2 * patches), 2 * patches)
        modes_t[half] = modes_ref[rows, :].T
    wait_bytes(spec.at[pl.ds(0, nb // nm)], sm_r.at[0])

    def partial(k, half):
        chip = pl.ds(pl.multiple_of(((here + half) % 2) * 2, 2), 2)
        return jnp.dot(
            modes_t[half], spec[k, chip].reshape(2 * patches, cols), preferred_element_type=jnp.float32)

    def y_copy(j):
        return to_band(part.at[2 * j + 1], summed.at[j], 1, ry_r.at[j], near)

    def z_copy(j):
        return to_band(part.at[2 * j], summed.at[pairs + j - 1], 1, rz_r.at[j - 1], band_at(2 * j))

    def pass_on(j, value):
        y_copy(j).wait_recv()
        part[2 * j] = (value + summed[j].astype(jnp.float32)).astype(jnp.bfloat16)
        z_copy(j).start()

    for i, e in enumerate(order):
        k = slot(i)
        own = partial(k, 0)
        s_cross(k).wait_recv()
        s_fwd(k).start()
        if e == 3:
            pass_on(3, pend[...])
        s_fwd(k).wait_recv()
        value = own + partial(k, 1)
        if e % 2:
            part[e] = value.astype(jnp.bfloat16)
            y_copy(e // 2).start()
        elif e == 6:
            pend[...] = value
        elif e:
            pass_on(e // 2, value)
        else:
            pend[...] = value
    loads[3].wait()
    res_t[...] = res_ref[...].astype(jnp.bfloat16).T
    loads[4].wait()
    total = pend[...]
    for j in range(pairs - 1, 0, -1):
        z_copy(j).wait_recv()
        total = total + summed[pairs + j - 1].astype(jnp.float32)
    y_copy(0).wait_recv()
    total = total + summed[0].astype(jnp.float32)
    kept = lax.broadcasted_iota(jnp.int32, (mode_cols, cols), 0) + m * mode_cols < rank_ref[...]
    total = jnp.where(kept, total, 0.0)
    coef[m] = total.astype(jnp.bfloat16)

    def k_copy(target):
        return to_mode(coef.at[m], coef.at[m], 2, k_r.at[0], target)

    for target in (cross, (mate + 2) % nm, mate):
        k_copy(target).start()
    wait_bytes(coef.at[pl.ds(0, nm - 1)], k_r.at[0])
    coefs = coef[...].reshape(nm * mode_cols, cols)
    forcing = jnp.dot(res_t[...], coefs, preferred_element_type=jnp.float32)
    forcing = jnp.where(kept, 2.0 * forcing, 0.0)
    force[b, m] = forcing.astype(jnp.bfloat16)

    half = mode_cols // 2
    upper, lower = pl.ds(0, half), pl.ds(half, half)

    def f_far(j):
        piece = force.at[b, m]
        return to_band(piece, piece, 5, far_r.at[j - 1], band_at(2 * j))

    def f_near(j, rows, sem):
        piece = force.at[band_at(2 * j), m, rows]
        return to_band(piece, piece, 4, sem.at[j], near)

    def f_cross(j, rows, sem):
        piece = force.at[band_at(2 * j), m, rows]
        return to_mode(piece, piece, 4, sem.at[j], cross)

    def g_near(j):
        piece = force.at[band_at(2 * j), cross, lower]
        return to_band(piece, piece, 4, g_r.at[j], near)

    def g_cross(j):
        piece = force.at[band_at(2 * j + 1), m, upper]
        return to_mode(piece, piece, 4, g_r.at[j], cross)

    def f_mate(e):
        piece = force.at[band_at(e), m]
        return to_mode(piece, piece, 4, mf_r.at[e], mate)

    def f_fwd(e):
        piece = force.at[band_at(e), cross]
        return to_mode(piece, piece, 4, mf_r.at[e], mate)

    def first(j):
        if j > 0:
            f_far(j).wait_recv()
        f_near(j, upper, nu_r).start()
        f_cross(j, lower, cl_r).start()
        f_near(j, lower, nl_r).start()
        f_cross(j, upper, cu_r).start()
        f_mate(2 * j).start()

    def second(j):
        f_near(j, upper, nu_r).wait_recv()
        g_cross(j).start()
        f_cross(j, lower, cl_r).wait_recv()
        g_near(j).start()
        f_near(j, lower, nl_r).wait_recv()
        f_mate(2 * j + 1).start()
        f_cross(j, upper, cu_r).wait_recv()
        f_fwd(2 * j).start()

    def third(j):
        wait_bytes(force.at[0, 0], g_r.at[j])
        f_fwd(2 * j + 1).start()

    for j in range(1, pairs):
        f_far(j).start()
    first(0)

    wait_bytes(basis.at[pl.ds(0, nm - 1)], ob_r.at[0])
    basis[m] = modes_ref[pl.ds(pl.multiple_of(m * patches, patches), patches), :]

    def surface(k):
        value = jnp.dot(basis[0], force[k, 0], preferred_element_type=jnp.float32)
        for j in range(1, nm):
            value = value + jnp.dot(basis[j], force[k, j], preferred_element_type=jnp.float32)
        return value.astype(jnp.bfloat16)

    def last(e):
        k = band_at(e)
        wait_bytes(force.at[0, pl.ds(0, 2)], mf_r.at[e])
        term = lax.dot_general(
            surface(k), table[k], (((1,), (1,)), ((), ())), preferred_element_type=jnp.float32)
        if e == 0:
            acc[...] = term
        elif e < nb - 1:
            acc[...] += term
        else:
            out_ref[...] = (acc[...] + term).astype(out_ref.dtype)

    second(0)
    first(1)
    first(2)
    last(0)
    third(0)
    first(3)
    last(1)
    second(1)
    last(2)
    second(2)
    third(1)
    last(4)
    second(3)
    last(3)
    third(2)
    last(6)
    third(3)
    last(5)
    last(7)

    wait_bytes(spec.at[pl.ds(0, nb - nb // nm)], tx.at[0])
    wait_bytes(part.at[pl.ds(0, nb - 1)], tx.at[1])
    wait_bytes(coef.at[pl.ds(0, nm - 1)], tx.at[2])
    wait_bytes(basis.at[pl.ds(0, nm - 1)], tx.at[3])
    wait_bytes(force.at[pl.ds(0, nb - 1)], tx.at[4])
    wait_bytes(force.at[0, pl.ds(0, pairs - 1)], tx.at[5])


def fused(mesh, velocity, radiation_modes, resistance, mode_ranks, freq_table):
    nb, nm = mesh.shape["band"], mesh.shape["mode"]
    patches, steps = velocity.shape[1:]
    mode_cols = radiation_modes.shape[1]
    modes = nm * mode_cols
    cols = 2 * (freq_table.shape[0] // nb)
    pairs = nb // 2
    bf16, f32 = jnp.bfloat16, jnp.float32
    sems = (5, 6, nb, 1, nb, pairs, pairs - 1, 1, 1, pairs - 1, pairs, pairs, pairs, pairs, pairs, nb)
    hbm = pl.BlockSpec(memory_space=pltpu.HBM)
    out = pl.pallas_call(
        functools.partial(fused_kernel, nb, nm),
        out_shape=pltpu.VMEM((patches, steps), bf16),
        in_specs=[hbm] * 5,
        out_specs=pl.BlockSpec(memory_space=pltpu.VMEM),
        scratch_shapes=[
            pltpu.VMEM((patches, steps), bf16),
            pltpu.VMEM(radiation_modes.shape, bf16),
            pltpu.VMEM(resistance.shape[1:], f32),
            pltpu.VMEM((1, 1), jnp.int32),
            pltpu.VMEM((pairs, cols), jnp.int32),
            pltpu.VMEM((nb, steps, cols), bf16),
            pltpu.VMEM((2, steps // HALF_ROWS, cols), f32),
            pltpu.VMEM((2, mode_cols, 2 * patches), bf16),
            pltpu.VMEM((mode_cols, modes), bf16),
            pltpu.VMEM((nb, nm, patches, cols), bf16),
            pltpu.VMEM((nb, mode_cols, cols), bf16),
            pltpu.VMEM((mode_cols, cols), f32),
            pltpu.VMEM((nb - 1, mode_cols, cols), bf16),
            pltpu.VMEM((nm, mode_cols, cols), bf16),
            pltpu.VMEM((nb, nm, mode_cols, cols), bf16),
            pltpu.VMEM((nm, patches, mode_cols), bf16),
            pltpu.VMEM((patches, steps), f32),
        ]
        + [pltpu.SemaphoreType.DMA((n,)) for n in sems],
        compiler_params=pltpu.CompilerParams(collective_id=0, has_side_effects=True),
    )(velocity[0], radiation_modes, resistance[0], mode_ranks.reshape(1, 1), freq_table.reshape(pairs, cols))
    return out[None]


def make_table(freq_table, step_count):
    times = jnp.arange(step_count, dtype=jnp.int32)
    phases = times[:, None] * freq_table[None, :] % step_count
    angles = phases.astype(jnp.float32) * (2.0 * math.pi / step_count)
    norming = 1.0 / math.sqrt(step_count)
    table = jnp.stack([jnp.cos(angles), -jnp.sin(angles)], axis=1) * norming
    return table.astype(jnp.bfloat16)


def add_sources(received):
    return jnp.sum(received, axis=0)


def per_device(velocity, radiation_modes, resistance, mode_ranks, freq_table):
    step_count = velocity.shape[2]
    mode_cols = radiation_modes.shape[1]
    dft_table = make_table(freq_table, step_count)
    spectra = jnp.einsum(
        "wpt,tcf->wpcf", velocity, dft_table, preferred_element_type=jnp.float32
    ).astype(jnp.bfloat16)
    partial_value = jnp.einsum(
        "wpcf,pr->wrcf",
        lax.all_gather(spectra, "mode", axis=1, tiled=True),
        radiation_modes,
        preferred_element_type=jnp.float32,
    )
    coefficients = add_sources(
        lax.all_to_all(
            partial_value[None].astype(jnp.bfloat16),
            "band",
            split_axis=4,
            concat_axis=0,
            tiled=True,
        ).astype(jnp.float32)
    )
    offset = lax.axis_index("mode") * mode_cols
    rank_here = mode_ranks[0]
    kept_mask = (offset + jnp.arange(mode_cols, dtype=jnp.int32) < rank_here).astype(jnp.float32)
    kept_mask = kept_mask[None, :, None, None]
    coefficients = coefficients * kept_mask
    matrix = resistance[0]
    partial_terms = jnp.einsum(
        "ij,wjcf->wicf", matrix, coefficients, precision=lax.Precision.HIGHEST
    )
    forcing = lax.psum_scatter(
        partial_terms.astype(jnp.bfloat16), "mode", scatter_dimension=1, tiled=True
    ).astype(jnp.float32)
    forcing = (2.0 * forcing * kept_mask).astype(jnp.bfloat16)
    collected = lax.all_gather(forcing, "mode", axis=1, tiled=True)
    collected = lax.all_gather(collected, "band", axis=3, tiled=True)
    own_basis = lax.all_to_all(radiation_modes, "mode", split_axis=0, concat_axis=1, tiled=True)
    surface_force = jnp.einsum(
        "pr,wrcf->wpcf", own_basis, collected, preferred_element_type=jnp.float32
    ).astype(jnp.bfloat16)
    history = jnp.einsum(
        "wpcf,tcf->wpt", surface_force, dft_table, preferred_element_type=jnp.float32
    )
    return history.astype(jnp.bfloat16)


def solution(mesh):
    placed = (
        P(None, ("band", "mode"), None),
        P("band", "mode"),
        P("band", None, "mode"),
        P("band"),
        P(),
    )
    nb, nm = mesh.shape["band"], mesh.shape["mode"]

    def body(velocity, radiation_modes, resistance, mode_ranks, freq_table):
        windows, patches, steps = velocity.shape
        mode_cols = radiation_modes.shape[1]
        cols = 2 * (freq_table.shape[0] // nb)
        tiled = (
            windows == 1 and nm == 4 and nb == 8 and cols == 128 and mode_cols % 128 == 0
            and patches % 128 == 0 and steps % 128 == 0 and steps & (steps - 1) == 0
        )
        args = (velocity, radiation_modes, resistance, mode_ranks, freq_table)
        return fused(mesh, *args) if tiled else per_device(*args)

    return jax.shard_map(
        body,
        mesh=mesh,
        in_specs=placed,
        out_specs=P(None, ("band", "mode"), None),
        check_vma=False,
    )
```

time: 48.2 us -> 46.2 us (0.959)
  the two profiles are of different devices: /device:TPU:0 before, /device:TPU:1 now
where the time goes in v2:
time: 46.2 us; the launch traced here: 46 us
  Pallas kernels  44.5 us (96%)
  local copies, waits for them, and re-layouts  0.8 us (2%)
  between operations  0.66 us (1%)
    pallas_call x1, Pallas kernels, fused(): pl.pallas_call(functools.partial(fused_kernel, nb, nm), out_shape=pltpu.V...  44.5 us

profile of v2, /device:TPU:1, one launch (start us, length us, event | category | flops | bytes accessed | tf_op | source)
XLA Modules:
  0.0 46.0 jit_solution(6986984954759469268)
XLA Ops:
  0.7 44.5 %shard_map.55 = bf16[256,1024]{1,0:T(8,128)(2,1)S(1)} custom-call(bf16[256,1024]{1,0:T(8,128)(2,1)} %bitcast.8, bf16[1024,256]{1,0:T(8,128)(2,1)} %modes_hbm.1, f32[1024,256]{1,0:T(8,128)} %bitcast.7, s32[1,1]{1,0:T(1,128)} %bitcast.5.rank_hbm, s32[4,128]{1,0:T(4,128)} %bitcast.9), custom_call_target="tpu_custom_call" | custom-call | tf_op jit(solution)/shard_map/pallas_call | solution.py:321
  45.2 0.8 %copy.7 = bf16[1,256,1024]{2,1,0:T(8,128)(2,1)} copy(bf16[1,256,1024]{2,1,0:T(8,128)(2,1)S(1)} %bitcast.6) | data formatting | bytes 1048576

commit v3 on v2

--- a/solution.py
+++ b/solution.py
@@ -31,7 +31,7 @@
     vel_ref, modes_ref, res_ref, rank_ref, freq_ref,
     table, trig, modes_t, res_t, spec, part, pend, summed, coef, force, basis, acc,
     in_s, tx, sx_r, sm_r, sf_r, ry_r, rz_r, k_r, ob_r,
-    far_r, nu_r, nl_r, cu_r, cl_r, g_r, mf_r,
+    far_r, nu_r, nl_r, cu_r, cl_r, g_r, h_r, mf_r,
 ):
     b = lax.axis_index("band")
     m = lax.axis_index("mode")
@@ -190,12 +190,22 @@
     total = jnp.where(kept, total, 0.0)
     coef[m] = total.astype(jnp.bfloat16)
 
-    def k_copy(target):
-        return to_mode(coef.at[m], coef.at[m], 2, k_r.at[0], target)
-
-    for target in (cross, (mate + 2) % nm, mate):
-        k_copy(target).start()
-    wait_bytes(coef.at[pl.ds(0, nm - 1)], k_r.at[0])
+    split = mode_cols * 5 // 8 // 16 * 16
+    head, tail = pl.ds(0, split), pl.ds(split, mode_cols - split)
+
+    def k_copy(source, rows, sem, target):
+        piece = coef.at[source, rows]
+        return to_mode(piece, piece, 2, k_r.at[sem], target)
+
+    k_copy(m, head, 0, cross).start()
+    k_copy(m, tail, 1, cross).start()
+    k_copy(m, tail, 2, (mate + 2) % nm).start()
+    k_copy(m, head, 3, mate).start()
+    k_copy(m, tail, 4, mate).start()
+    k_copy(cross, head, 0, cross).wait_recv()
+    k_copy(cross, head, 5, mate).start()
+    for rows, sem in ((tail, 1), (tail, 2), (head, 3), (tail, 4), (head, 5)):
+        k_copy(m, rows, sem, mate).wait_recv()
     coefs = coef[...].reshape(nm * mode_cols, cols)
     forcing = jnp.dot(res_t[...], coefs, preferred_element_type=jnp.float32)
     forcing = jnp.where(kept, 2.0 * forcing, 0.0)
@@ -224,6 +234,20 @@
         piece = force.at[band_at(2 * j + 1), m, upper]
         return to_mode(piece, piece, 4, g_r.at[j], cross)
 
+    def f_diag(j):
+        piece = force.at[band_at(2 * j), m]
+        return pltpu.make_async_remote_copy(
+            src_ref=piece, dst_ref=piece, send_sem=tx.at[4], recv_sem=g_r.at[j],
+            device_id={"band": near, "mode": cross}, device_id_type=MESH)
+
+    def h_near():
+        piece = force.at[near, m]
+        return to_band(piece, piece, 4, h_r.at[0], band_at(2))
+
+    def h_cross():
+        piece = force.at[b, cross]
+        return to_band(piece, piece, 4, h_r.at[1], band_at(2))
+
     def f_mate(e):
         piece = force.at[band_at(e), m]
         return to_mode(piece, piece, 4, mf_r.at[e], mate)
@@ -232,32 +256,51 @@
         piece = force.at[band_at(e), cross]
         return to_mode(piece, piece, 4, mf_r.at[e], mate)
 
+    def arrived(j):
+        f_far(j).wait_recv()
+
     def first(j):
-        if j > 0:
-            f_far(j).wait_recv()
-        f_near(j, upper, nu_r).start()
-        f_cross(j, lower, cl_r).start()
-        f_near(j, lower, nl_r).start()
-        f_cross(j, upper, cu_r).start()
+        if j != 1:
+            f_near(j, upper, nu_r).start()
+            f_cross(j, lower, cl_r).start()
+            f_near(j, lower, nl_r).start()
+            f_cross(j, upper, cu_r).start()
         f_mate(2 * j).start()
 
     def second(j):
+        if j == 1:
+            h_near().wait_recv()
+            g_cross(j).start()
+            f_mate(2 * j + 1).start()
+            h_cross().wait_recv()
+            g_near(j).start()
+            f_fwd(2 * j).start()
+            return
         f_near(j, upper, nu_r).wait_recv()
-        g_cross(j).start()
+        if j:
+            g_cross(j).start()
         f_cross(j, lower, cl_r).wait_recv()
-        g_near(j).start()
+        if j:
+            g_near(j).start()
+
+    def settle(j):
         f_near(j, lower, nl_r).wait_recv()
+        if j == 0:
+            h_near().start()
         f_mate(2 * j + 1).start()
         f_cross(j, upper, cu_r).wait_recv()
+        if j == 0:
+            h_cross().start()
         f_fwd(2 * j).start()
 
     def third(j):
         wait_bytes(force.at[0, 0], g_r.at[j])
         f_fwd(2 * j + 1).start()
 
-    for j in range(1, pairs):
+    first(0)
+    f_diag(0).start()
+    for j in (1, 2, 3):
         f_far(j).start()
-    first(0)
 
     wait_bytes(basis.at[pl.ds(0, nm - 1)], ob_r.at[0])
     basis[m] = modes_ref[pl.ds(pl.multiple_of(m * patches, patches), patches), :]
@@ -268,38 +311,43 @@
             value = value + jnp.dot(basis[j], force[k, j], preferred_element_type=jnp.float32)
         return value.astype(jnp.bfloat16)
 
-    def last(e):
+    def last(e, place=1):
         k = band_at(e)
         wait_bytes(force.at[0, pl.ds(0, 2)], mf_r.at[e])
         term = lax.dot_general(
             surface(k), table[k], (((1,), (1,)), ((), ())), preferred_element_type=jnp.float32)
-        if e == 0:
+        if place == 0:
             acc[...] = term
-        elif e < nb - 1:
+        elif place == 1:
             acc[...] += term
         else:
             out_ref[...] = (acc[...] + term).astype(out_ref.dtype)
 
     second(0)
+    settle(0)
+    arrived(2)
+    first(2)
+    arrived(1)
     first(1)
-    first(2)
-    last(0)
     third(0)
+    last(0, 0)
+    arrived(3)
     first(3)
-    last(1)
+    last(1, 1)
+    second(2)
+    settle(2)
     second(1)
-    last(2)
-    second(2)
+    second(3)
+    settle(3)
+    third(2)
+    last(4, 1)
+    last(2, 1)
     third(1)
-    last(4)
-    second(3)
-    last(3)
-    third(2)
-    last(6)
+    last(6, 1)
     third(3)
-    last(5)
-    last(7)
-
+    last(5, 1)
+    last(3, 1)
+    last(7, 2)
     wait_bytes(spec.at[pl.ds(0, nb - nb // nm)], tx.at[0])
     wait_bytes(part.at[pl.ds(0, nb - 1)], tx.at[1])
     wait_bytes(coef.at[pl.ds(0, nm - 1)], tx.at[2])
@@ -316,7 +364,7 @@
     cols = 2 * (freq_table.shape[0] // nb)
     pairs = nb // 2
     bf16, f32 = jnp.bfloat16, jnp.float32
-    sems = (5, 6, nb, 1, nb, pairs, pairs - 1, 1, 1, pairs - 1, pairs, pairs, pairs, pairs, pairs, nb)
+    sems = (5, 6, nb, 1, nb, pairs, pairs - 1, 6, 1, pairs - 1, pairs, pairs, pairs, pairs, pairs, 2, nb)
     hbm = pl.BlockSpec(memory_space=pltpu.HBM)
     out = pl.pallas_call(
         functools.partial(fused_kernel, nb, nm),

time: 46.2 us -> 44.6 us (0.965)
  the two profiles are of different devices: /device:TPU:1 before, /device:TPU:0 now
where the time goes in v3:
time: 44.6 us; the launch traced here: 44.4 us
  Pallas kernels  42.9 us (96%)
  local copies, waits for them, and re-layouts  0.8 us (2%)
  between operations  0.66 us (1%)
    pallas_call x1, Pallas kernels, fused(): pl.pallas_call(functools.partial(fused_kernel, nb, nm), out_shape=pltpu.V...  42.9 us

profile of v3, /device:TPU:0, one launch (start us, length us, event | category | flops | bytes accessed | tf_op | source)
XLA Modules:
  0.0 44.4 jit_solution(9692356332391566868)
XLA Ops:
  0.7 42.9 %shard_map.55 = bf16[256,1024]{1,0:T(8,128)(2,1)S(1)} custom-call(bf16[256,1024]{1,0:T(8,128)(2,1)} %bitcast.8, bf16[1024,256]{1,0:T(8,128)(2,1)} %modes_hbm.1, f32[1024,256]{1,0:T(8,128)} %bitcast.7, s32[1,1]{1,0:T(1,128)} %bitcast.5.rank_hbm, s32[4,128]{1,0:T(4,128)} %bitcast.9), custom_call_target="tpu_custom_call" | custom-call | tf_op jit(solution)/shard_map/pallas_call | solution.py:369
  43.6 0.8 %copy.7 = bf16[1,256,1024]{2,1,0:T(8,128)(2,1)} copy(bf16[1,256,1024]{2,1,0:T(8,128)(2,1)S(1)} %bitcast.6) | data formatting | bytes 1048576

commit v4 on v3

--- a/solution.py
+++ b/solution.py
@@ -30,7 +30,7 @@
     nb, nm, vel_hbm, modes_hbm, res_hbm, rank_hbm, freq_hbm, out_ref,
     vel_ref, modes_ref, res_ref, rank_ref, freq_ref,
     table, trig, modes_t, res_t, spec, part, pend, summed, coef, force, basis, acc,
-    in_s, tx, sx_r, sm_r, sf_r, ry_r, rz_r, k_r, ob_r,
+    ready, in_s, tx, sx_r, sm_r, sf_r, ry_r, rz_r, k_r, ob_r,
     far_r, nu_r, nl_r, cu_r, cl_r, g_r, h_r, mf_r,
 ):
     b = lax.axis_index("band")
@@ -42,6 +42,7 @@
     cols = table.shape[2]
     mode_cols = modes_ref.shape[1]
     pairs = nb // 2
+    inner = (b // 2 + 1) // 2 % 2
 
     def band_at(e):
         bits = [1 << i for i in range(nb.bit_length() - 1)]
@@ -73,8 +74,12 @@
     barrier = pltpu.get_barrier_semaphore()
     for off in range(1, nm):
         pl.semaphore_signal(barrier, inc=1, device_id={"mode": (m + off) % nm}, device_id_type=MESH)
-    for off in range(1, nb):
+    for off in (1, 2):
         pl.semaphore_signal(barrier, inc=1, device_id={"band": band_at(off)}, device_id_type=MESH)
+
+    @pl.when(inner == 1)
+    def _():
+        pl.semaphore_signal(barrier, inc=1, device_id={"band": band_at(6)}, device_id_type=MESH)
 
     blocks = steps // HALF_ROWS
     norming = 1.0 / math.sqrt(steps)
@@ -121,7 +126,11 @@
     build(slot(0))
     loads[1].wait()
     project(slot(0))
-    pl.semaphore_wait(barrier, nm - 1 + nb - 1)
+    pl.semaphore_wait(barrier, nm + 1 + inner)
+
+    @pl.when(inner == 1)
+    def _():
+        pl.semaphore_signal(ready, inc=1, device_id={"band": band_at(6)}, device_id_type=MESH)
 
     for i in range(nb):
         s_cross(slot(i)).start()
@@ -138,6 +147,12 @@
     loads[2].wait()
     for off in range(1, nm):
         basis_copy(off).start()
+
+    @pl.when(inner == 1)
+    def _():
+        pl.semaphore_wait(ready, 1)
+        pl.semaphore_signal(ready, inc=1, device_id={"band": band_at(2)}, device_id_type=MESH)
+
     for half in range(2):
         rows = pl.ds(pl.multiple_of(((here + half) % 2) * 2 * patches, 2 * patches), 2 * patches)
         modes_t[half] = modes_ref[rows, :].T
@@ -165,6 +180,10 @@
         s_cross(k).wait_recv()
         s_fwd(k).start()
         if e == 3:
+            @pl.when(inner == 0)
+            def _():
+                pl.semaphore_wait(ready, 1)
+
             pass_on(3, pend[...])
         s_fwd(k).wait_recv()
         value = own + partial(k, 1)
@@ -390,6 +409,7 @@
             pltpu.VMEM((nm, patches, mode_cols), bf16),
             pltpu.VMEM((patches, steps), f32),
         ]
+        + [pltpu.SemaphoreType.REGULAR]
         + [pltpu.SemaphoreType.DMA((n,)) for n in sems],
         compiler_params=pltpu.CompilerParams(collective_id=0, has_side_effects=True),
     )(velocity[0], radiation_modes, resistance[0], mode_ranks.reshape(1, 1), freq_table.reshape(pairs, cols))

time: 44.6 us -> 43.6 us (0.978)
  Pallas kernels: 42.9 us -> 41.9 us
    pallas_call x1, Pallas kernels: 42.9 us -> 41.9 us  [fused(): pl.pallas_call(functools.partial(fused_kernel, nb, nm), out_shape=pltpu.V...]
where the time goes in v4:
time: 43.6 us; the launch traced here: 43.4 us
  Pallas kernels  41.9 us (96%)
  local copies, waits for them, and re-layouts  0.8 us (2%)
  between operations  0.66 us (2%)
    pallas_call x1, Pallas kernels, fused(): pl.pallas_call(functools.partial(fused_kernel, nb, nm), out_shape=pltpu.V...  41.9 us

profile of v4, /device:TPU:0, one launch (start us, length us, event | category | flops | bytes accessed | tf_op | source)
XLA Modules:
  0.0 43.4 jit_solution(11227578271884344243)
XLA Ops:
  0.7 41.9 %shard_map.55 = bf16[256,1024]{1,0:T(8,128)(2,1)S(1)} custom-call(bf16[256,1024]{1,0:T(8,128)(2,1)} %bitcast.8, bf16[1024,256]{1,0:T(8,128)(2,1)} %modes_hbm.1, f32[1024,256]{1,0:T(8,128)} %bitcast.7, s32[1,1]{1,0:T(1,128)} %bitcast.5.rank_hbm, s32[4,128]{1,0:T(4,128)} %bitcast.9), custom_call_target="tpu_custom_call" | custom-call | tf_op jit(solution)/shard_map/pallas_call | solution.py:388
  42.6 0.8 %copy.7 = bf16[1,256,1024]{2,1,0:T(8,128)(2,1)} copy(bf16[1,256,1024]{2,1,0:T(8,128)(2,1)S(1)} %bitcast.6) | data formatting | bytes 1048576

commit v5 on v4

--- a/solution.py
+++ b/solution.py
@@ -318,8 +318,13 @@
 
     first(0)
     f_diag(0).start()
-    for j in (1, 2, 3):
-        f_far(j).start()
+    f_far(1).start()
+    f_far(3 - inner).start()
+
+    @pl.when(inner == 0)
+    def _():
+        f_far(2).start()
+
 
     wait_bytes(basis.at[pl.ds(0, nm - 1)], ob_r.at[0])
     basis[m] = modes_ref[pl.ds(pl.multiple_of(m * patches, patches), patches), :]
@@ -343,6 +348,11 @@
             out_ref[...] = (acc[...] + term).astype(out_ref.dtype)
 
     second(0)
+
+    @pl.when(inner == 1)
+    def _():
+        f_far(3).start()
+
     settle(0)
     arrived(2)
     first(2)
@@ -367,6 +377,7 @@
     last(5, 1)
     last(3, 1)
     last(7, 2)
+
     wait_bytes(spec.at[pl.ds(0, nb - nb // nm)], tx.at[0])
     wait_bytes(part.at[pl.ds(0, nb - 1)], tx.at[1])
     wait_bytes(coef.at[pl.ds(0, nm - 1)], tx.at[2])

time: 43.6 us -> 43.2 us (level)
  the two profiles are of different devices: /device:TPU:0 before, /device:TPU:9 now
where the time goes in v5:
time: 43.2 us; the launch traced here: 43 us
  Pallas kernels  41.6 us (96%)
  local copies, waits for them, and re-layouts  0.8 us (2%)
  between operations  0.66 us (2%)
    pallas_call x1, Pallas kernels, fused(): pl.pallas_call(functools.partial(fused_kernel, nb, nm), out_shape=pltpu.V...  41.6 us

profile of v5, /device:TPU:9, one launch (start us, length us, event | category | flops | bytes accessed | tf_op | source)
XLA Modules:
  0.0 43.0 jit_solution(3595942809743501844)
XLA Ops:
  0.7 41.6 %shard_map.55 = bf16[256,1024]{1,0:T(8,128)(2,1)S(1)} custom-call(bf16[256,1024]{1,0:T(8,128)(2,1)} %bitcast.8, bf16[1024,256]{1,0:T(8,128)(2,1)} %modes_hbm.1, f32[1024,256]{1,0:T(8,128)} %bitcast.7, s32[1,1]{1,0:T(1,128)} %bitcast.5.rank_hbm, s32[4,128]{1,0:T(4,128)} %bitcast.9), custom_call_target="tpu_custom_call" | custom-call | tf_op jit(solution)/shard_map/pallas_call | solution.py:399
  42.2 0.8 %copy.7 = bf16[1,256,1024]{2,1,0:T(8,128)(2,1)} copy(bf16[1,256,1024]{2,1,0:T(8,128)(2,1)S(1)} %bitcast.6) | data formatting | bytes 1048576

commit v6 on v5

--- a/solution.py
+++ b/solution.py
@@ -326,6 +326,10 @@
         f_far(2).start()
 
 
+    @pl.when(inner == 1)
+    def _():
+        f_far(3).start()
+
     wait_bytes(basis.at[pl.ds(0, nm - 1)], ob_r.at[0])
     basis[m] = modes_ref[pl.ds(pl.multiple_of(m * patches, patches), patches), :]
 
@@ -348,11 +352,6 @@
             out_ref[...] = (acc[...] + term).astype(out_ref.dtype)
 
     second(0)
-
-    @pl.when(inner == 1)
-    def _():
-        f_far(3).start()
-
     settle(0)
     arrived(2)
     first(2)

time: 43.2 us -> 43 us (level)
  no operation moved by 1% of the time
where the time goes in v6:
time: 43 us; the launch traced here: 42.9 us
  Pallas kernels  41.4 us (96%)
  local copies, waits for them, and re-layouts  0.8 us (2%)
  between operations  0.66 us (2%)
    pallas_call x1, Pallas kernels, fused(): pl.pallas_call(functools.partial(fused_kernel, nb, nm), out_shape=pltpu.V...  41.4 us

profile of v6, /device:TPU:9, one launch (start us, length us, event | category | flops | bytes accessed | tf_op | source)
XLA Modules:
  0.0 42.9 jit_solution(10293251919097488489)
XLA Ops:
  0.7 41.4 %shard_map.55 = bf16[256,1024]{1,0:T(8,128)(2,1)S(1)} custom-call(bf16[256,1024]{1,0:T(8,128)(2,1)} %bitcast.8, bf16[1024,256]{1,0:T(8,128)(2,1)} %modes_hbm.1, f32[1024,256]{1,0:T(8,128)} %bitcast.7, s32[1,1]{1,0:T(1,128)} %bitcast.5.rank_hbm, s32[4,128]{1,0:T(4,128)} %bitcast.9), custom_call_target="tpu_custom_call" | custom-call | tf_op jit(solution)/shard_map/pallas_call | solution.py:398
  42.1 0.8 %copy.7 = bf16[1,256,1024]{2,1,0:T(8,128)(2,1)} copy(bf16[1,256,1024]{2,1,0:T(8,128)(2,1)S(1)} %bitcast.6) | data formatting | bytes 1048576

commit v7 on v5

--- a/solution.py
+++ b/solution.py
@@ -216,17 +216,23 @@
         piece = coef.at[source, rows]
         return to_mode(piece, piece, 2, k_r.at[sem], target)
 
+    def product(half):
+        chip = ((here + half) % 2) * 2
+        part_t = res_t[:, pl.ds(pl.multiple_of(chip * mode_cols, 2 * mode_cols), 2 * mode_cols)]
+        rows = coef[pl.ds(chip, 2)].reshape(2 * mode_cols, cols)
+        return jnp.dot(part_t, rows, preferred_element_type=jnp.float32)
+
     k_copy(m, head, 0, cross).start()
     k_copy(m, tail, 1, cross).start()
-    k_copy(m, tail, 2, (mate + 2) % nm).start()
-    k_copy(m, head, 3, mate).start()
-    k_copy(m, tail, 4, mate).start()
+    k_copy(m, tail, 1, (mate + 2) % nm).start()
+    k_copy(m, pl.ds(0, mode_cols), 2, mate).start()
     k_copy(cross, head, 0, cross).wait_recv()
-    k_copy(cross, head, 5, mate).start()
-    for rows, sem in ((tail, 1), (tail, 2), (head, 3), (tail, 4), (head, 5)):
-        k_copy(m, rows, sem, mate).wait_recv()
-    coefs = coef[...].reshape(nm * mode_cols, cols)
-    forcing = jnp.dot(res_t[...], coefs, preferred_element_type=jnp.float32)
+    k_copy(cross, head, 3, mate).start()
+    k_copy(m, pl.ds(0, mode_cols), 2, mate).wait_recv()
+    forcing = product(0)
+    wait_bytes(coef.at[0, pl.ds(0, 2 * (mode_cols - split))], k_r.at[1])
+    k_copy(m, head, 3, mate).wait_recv()
+    forcing = forcing + product(1)
     forcing = jnp.where(kept, 2.0 * forcing, 0.0)
     force[b, m] = forcing.astype(jnp.bfloat16)
 
@@ -394,7 +400,7 @@
     cols = 2 * (freq_table.shape[0] // nb)
     pairs = nb // 2
     bf16, f32 = jnp.bfloat16, jnp.float32
-    sems = (5, 6, nb, 1, nb, pairs, pairs - 1, 6, 1, pairs - 1, pairs, pairs, pairs, pairs, pairs, 2, nb)
+    sems = (5, 6, nb, 1, nb, pairs, pairs - 1, 4, 1, pairs - 1, pairs, pairs, pairs, pairs, pairs, 2, nb)
     hbm = pl.BlockSpec(memory_space=pltpu.HBM)
     out = pl.pallas_call(
         functools.partial(fused_kernel, nb, nm),

time: 43.2 us -> 43.2 us (level)
  no operation moved by 1% of the time
where the time goes in v7:
time: 43.2 us; the launch traced here: 43 us
  Pallas kernels  41.5 us (96%)
  local copies, waits for them, and re-layouts  0.8 us (2%)
  between operations  0.66 us (2%)
    pallas_call x1, Pallas kernels, fused(): pl.pallas_call(functools.partial(fused_kernel, nb, nm), out_shape=pltpu.V...  41.5 us

profile of v7, /device:TPU:9, one launch (start us, length us, event | category | flops | bytes accessed | tf_op | source)
XLA Modules:
  0.0 43.0 jit_solution(18260584625751267395)
XLA Ops:
  0.7 41.5 %shard_map.55 = bf16[256,1024]{1,0:T(8,128)(2,1)S(1)} custom-call(bf16[256,1024]{1,0:T(8,128)(2,1)} %bitcast.8, bf16[1024,256]{1,0:T(8,128)(2,1)} %modes_hbm.1, f32[1024,256]{1,0:T(8,128)} %bitcast.7, s32[1,1]{1,0:T(1,128)} %bitcast.5.rank_hbm, s32[4,128]{1,0:T(4,128)} %bitcast.9), custom_call_target="tpu_custom_call" | custom-call | tf_op jit(solution)/shard_map/pallas_call | solution.py:405
  42.2 0.8 %copy.7 = bf16[1,256,1024]{2,1,0:T(8,128)(2,1)} copy(bf16[1,256,1024]{2,1,0:T(8,128)(2,1)S(1)} %bitcast.6) | data formatting | bytes 1048576

commit v8 on v6

--- a/solution.py
+++ b/solution.py
@@ -278,8 +278,13 @@
     def arrived(j):
         f_far(j).wait_recv()
 
+    whole = pl.ds(0, mode_cols)
+
     def first(j):
-        if j != 1:
+        if j == 0:
+            f_near(j, whole, nl_r).start()
+            f_cross(j, whole, cu_r).start()
+        elif j != 1:
             f_near(j, upper, nu_r).start()
             f_cross(j, lower, cl_r).start()
             f_near(j, lower, nl_r).start()
@@ -302,12 +307,19 @@
         if j:
             g_near(j).start()
 
+    def late():
+        @pl.when(inner == 1)
+        def _():
+            f_far(3).start()
+
     def settle(j):
-        f_near(j, lower, nl_r).wait_recv()
+        rows_n, rows_c = (lower, upper) if j else (whole, whole)
+        f_near(j, rows_n, nl_r).wait_recv()
         if j == 0:
+            late()
             h_near().start()
         f_mate(2 * j + 1).start()
-        f_cross(j, upper, cu_r).wait_recv()
+        f_cross(j, rows_c, cu_r).wait_recv()
         if j == 0:
             h_cross().start()
         f_fwd(2 * j).start()
@@ -325,10 +337,6 @@
     def _():
         f_far(2).start()
 
-
-    @pl.when(inner == 1)
-    def _():
-        f_far(3).start()
 
     wait_bytes(basis.at[pl.ds(0, nm - 1)], ob_r.at[0])
     basis[m] = modes_ref[pl.ds(pl.multiple_of(m * patches, patches), patches), :]
@@ -351,7 +359,6 @@
         else:
             out_ref[...] = (acc[...] + term).astype(out_ref.dtype)
 
-    second(0)
     settle(0)
     arrived(2)
     first(2)

time: 43 us -> 43.2 us (level)
  no operation moved by 1% of the time
where the time goes in v8:
time: 43.2 us; the launch traced here: 43 us
  Pallas kernels  41.6 us (96%)
  local copies, waits for them, and re-layouts  0.8 us (2%)
  between operations  0.66 us (2%)
    pallas_call x1, Pallas kernels, fused(): pl.pallas_call(functools.partial(fused_kernel, nb, nm), out_shape=pltpu.V...  41.6 us

profile of v8, /device:TPU:9, one launch (start us, length us, event | category | flops | bytes accessed | tf_op | source)
XLA Modules:
  0.0 43.0 jit_solution(2527560562265139718)
XLA Ops:
  0.7 41.6 %shard_map.55 = bf16[256,1024]{1,0:T(8,128)(2,1)S(1)} custom-call(bf16[256,1024]{1,0:T(8,128)(2,1)} %bitcast.8, bf16[1024,256]{1,0:T(8,128)(2,1)} %modes_hbm.1, f32[1024,256]{1,0:T(8,128)} %bitcast.7, s32[1,1]{1,0:T(1,128)} %bitcast.5.rank_hbm, s32[4,128]{1,0:T(4,128)} %bitcast.9), custom_call_target="tpu_custom_call" | custom-call | tf_op jit(solution)/shard_map/pallas_call | solution.py:405
  42.2 0.8 %copy.7 = bf16[1,256,1024]{2,1,0:T(8,128)(2,1)} copy(bf16[1,256,1024]{2,1,0:T(8,128)(2,1)S(1)} %bitcast.6) | data formatting | bytes 1048576

commit v9 on v6

--- a/solution.py
+++ b/solution.py
@@ -233,8 +233,8 @@
     half = mode_cols // 2
     upper, lower = pl.ds(0, half), pl.ds(half, half)
 
-    def f_far(j):
-        piece = force.at[b, m]
+    def f_far(j, rows=pl.ds(0, mode_cols)):
+        piece = force.at[b, m, rows]
         return to_band(piece, piece, 5, far_r.at[j - 1], band_at(2 * j))
 
     def f_near(j, rows, sem):
@@ -328,7 +328,7 @@
 
     @pl.when(inner == 1)
     def _():
-        f_far(3).start()
+        f_far(3, upper).start()
 
     wait_bytes(basis.at[pl.ds(0, nm - 1)], ob_r.at[0])
     basis[m] = modes_ref[pl.ds(pl.multiple_of(m * patches, patches), patches), :]
@@ -352,11 +352,16 @@
             out_ref[...] = (acc[...] + term).astype(out_ref.dtype)
 
     second(0)
+
+    @pl.when(inner == 1)
+    def _():
+        f_far(3, lower).start()
+
     settle(0)
+    arrived(1)
+    first(1)
     arrived(2)
     first(2)
-    arrived(1)
-    first(1)
     third(0)
     last(0, 0)
     arrived(3)

time: 43 us -> 43 us (level)
  no operation moved by 1% of the time
where the time goes in v9:
time: 43 us; the launch traced here: 42.9 us
  Pallas kernels  41.4 us (96%)
  local copies, waits for them, and re-layouts  0.8 us (2%)
  between operations  0.66 us (2%)
    pallas_call x1, Pallas kernels, fused(): pl.pallas_call(functools.partial(fused_kernel, nb, nm), out_shape=pltpu.V...  41.4 us

profile of v9, /device:TPU:9, one launch (start us, length us, event | category | flops | bytes accessed | tf_op | source)
XLA Modules:
  0.0 42.9 jit_solution(17062041846555811806)
XLA Ops:
  0.7 41.4 %shard_map.55 = bf16[256,1024]{1,0:T(8,128)(2,1)S(1)} custom-call(bf16[256,1024]{1,0:T(8,128)(2,1)} %bitcast.8, bf16[1024,256]{1,0:T(8,128)(2,1)} %modes_hbm.1, f32[1024,256]{1,0:T(8,128)} %bitcast.7, s32[1,1]{1,0:T(1,128)} %bitcast.5.rank_hbm, s32[4,128]{1,0:T(4,128)} %bitcast.9), custom_call_target="tpu_custom_call" | custom-call | tf_op jit(solution)/shard_map/pallas_call | solution.py:403
  42.1 0.8 %copy.7 = bf16[1,256,1024]{2,1,0:T(8,128)(2,1)} copy(bf16[1,256,1024]{2,1,0:T(8,128)(2,1)S(1)} %bitcast.6) | data formatting | bytes 1048576
